TPU v7x, 128 devices: a whole 4x4x4 slice. The times are simulated.
128 devices in a mesh: req: 16 (over z, x), tok: 8 (over y, core).
Axes of the slice: x: 4, y: 4, z: 4, core: 2. Of those that a mesh axis runs over, the one named last changes fastest.
Arguments:
- queries: bfloat16 [8192, 2048], P('req', 'tok'), may hold values from -6 to 6
- suffix_kv: bfloat16 [8192, 2048], P('req'), may hold values from -6 to 6
- prefix_cache: bfloat16 [8192, 2048], P('req'), may hold values from -24 to 24
- q_gain: float32 [256], replicated, may hold values from 0.1 to 1.9
- k_gain: float32 [256], replicated, may hold values from 0.1 to 1.9
- lengths: int32 [16, 3], P('req'), may hold values from 1 to 256, 512 in all within a row
- group_of: int32 [16], replicated, may hold values from 0 to 1
- owner_order: int32 [16], replicated, may hold values from 0 to 15, each once
- residual: bfloat16 [8192, 2560], P('req'), may hold values from -6 to 6
- w_out: bfloat16 [2048, 2560], P('tok'), may hold values from -0.125 to 0.125
- attn_gain: float32 [2560], replicated, may hold values from 0.1 to 1.9
- ffn_in_gain: float32 [2560], replicated, may hold values from 0.1 to 1.9
- ffn_out_gain: float32 [2560], replicated, may hold values from 0.1 to 1.9
- w_gate: bfloat16 [2560, 10240], P(None, 'tok'), may hold values from -0.125 to 0.125
- w_up: bfloat16 [2560, 10240], P(None, 'tok'), may hold values from -0.125 to 0.125
- w_down: bfloat16 [10240, 2560], P('tok'), may hold values from -0.0625 to 0.0625
Outputs:
- layer_out: bfloat16 [8192, 2560], P(('req', 'tok'))
Inputs may be any that keep to these rules, and one draw needn't show every extreme that they name: The 3 lengths of each req index sum to 512; the largest is exactly 256. `owner_order`: each req index appears once; entries g * 8 to g * 8 + 7 name the holders of group g's prefix.
All inputs are finite; a program needn't handle non-finite values.
Results may differ from a plain program's by a relative error of at most 0.02.
Values may be sent and summed in bfloat16 or wider, within the bound.
A program may use at most 128 MiB of HBM per device.

v0:
```python
import jax
import jax.numpy as jnp
from jax import lax
from jax.sharding import PartitionSpec as P

H = 8
KVH = 4
HD = 256
GROUPS = 2
EPSILON = 1e-06
MASKED = -1e30


def rms_scale(values_in, gain_vec):
    return (
        values_in
        * lax.rsqrt(jnp.mean(values_in * values_in, axis=-1, keepdims=True) + EPSILON)
        * gain_vec
    )


def norm_heads(values_in, gain_vec, head_count):
    row_count = values_in.shape[0]
    shaped = values_in.astype(jnp.float32).reshape(row_count, head_count, HD)
    return rms_scale(shaped, gain_vec).astype(jnp.bfloat16).reshape(row_count, head_count * HD)


def local(
    queries,
    suffix_kv,
    prefix_cache,
    q_gain,
    k_gain,
    lengths,
    group_of,
    owner_order,
    residual,
    w_out,
    attn_gain,
    ffn_in_gain,
    ffn_out_gain,
    w_gate,
    w_up,
    w_down,
):
    req_count = lax.axis_size("req")
    tok_count = lax.axis_size("tok")
    req_index = lax.axis_index("req")
    tok_index = lax.axis_index("tok")
    row_count = queries.shape[0]
    heads_here = queries.shape[1] // HD
    head_ratio = H // KVH
    kv_first = tok_index * heads_here // head_ratio
    kv_width = KVH * HD
    own_count = req_count // GROUPS
    with jax.named_scope("prefix_gather"):
        pref_keys = lax.dynamic_slice_in_dim(prefix_cache, kv_first * HD, HD, 1)
        pref_vals = lax.dynamic_slice_in_dim(prefix_cache, kv_width + kv_first * HD, HD, 1)
        pref_kv = jnp.concatenate([pref_keys, pref_vals], axis=1)
        gathered = lax.all_gather(pref_kv, "req", axis=0, tiled=False)
        own_group = group_of[req_index]
        owner_ids = lax.dynamic_slice_in_dim(owner_order, own_group * own_count, own_count)
        shared = jnp.take(gathered, owner_ids, axis=0).reshape(-1, 2 * HD)
    with jax.named_scope("attention"):
        query_normed = norm_heads(queries, q_gain, heads_here)
        suf_keys = norm_heads(lax.dynamic_slice_in_dim(suffix_kv, kv_first * HD, HD, 1), k_gain, 1)
        suf_vals = lax.dynamic_slice_in_dim(suffix_kv, kv_width + kv_first * HD, HD, 1)
        all_keys = jnp.concatenate([shared[:, :HD], suf_keys], axis=0)
        all_vals = jnp.concatenate([shared[:, HD:], suf_vals], axis=0)
        seg_ends = jnp.cumsum(lengths[0])
        positions = jnp.arange(row_count, dtype=jnp.int32)
        segment = jnp.sum((positions[:, None] >= seg_ends[None, :]).astype(jnp.int32), axis=1)
        causal = (segment[:, None] == segment[None, :]) & (positions[None, :] <= positions[:, None])
        visible = jnp.concatenate(
            [jnp.ones((row_count, shared.shape[0]), jnp.bool_), causal], axis=1
        )
        outputs = []
        for head_idx in range(heads_here):
            head_q = query_normed[:, head_idx * HD : (head_idx + 1) * HD]
            scores = jnp.dot(head_q, all_keys.T, preferred_element_type=jnp.float32) * HD ** (-0.5)
            scores = jnp.where(visible, scores, MASKED)
            row_max = jnp.max(scores, axis=-1, keepdims=True)
            weights = jnp.exp(scores - row_max)
            row_sum = jnp.sum(weights, axis=-1, keepdims=True)
            head_out = (
                jnp.dot(weights.astype(jnp.bfloat16), all_vals, preferred_element_type=jnp.float32)
                / row_sum
            )
            outputs.append(head_out)
        attention = jnp.concatenate(outputs, axis=1).astype(jnp.bfloat16)
    share = row_count // tok_count
    first_row = tok_index * share
    with jax.named_scope("out_projection"):
        projected = lax.psum_scatter(
            jnp.dot(attention, w_out, preferred_element_type=jnp.float32),
            "tok",
            scatter_dimension=0,
            tiled=True,
        )
        residual_share = lax.dynamic_slice_in_dim(residual, first_row, share, 0)
        mixed_share = residual_share.astype(jnp.float32) + rms_scale(projected, attn_gain)
        normed_share = rms_scale(mixed_share, ffn_in_gain).astype(jnp.bfloat16)
        normed = lax.all_gather(normed_share, "tok", axis=0, tiled=True)
    with jax.named_scope("feed_forward"):
        gate = jnp.dot(normed, w_gate, preferred_element_type=jnp.float32)
        upward = jnp.dot(normed, w_up, preferred_element_type=jnp.float32)
        hidden = (jax.nn.gelu(gate, approximate=True) * upward).astype(jnp.bfloat16)
        down_share = lax.psum_scatter(
            jnp.dot(hidden, w_down, preferred_element_type=jnp.float32),
            "tok",
            scatter_dimension=0,
            tiled=True,
        )
    return (mixed_share + rms_scale(down_share, ffn_out_gain)).astype(jnp.bfloat16)


def solution(mesh):
    in_specs = (
        P("req", "tok"),
        P("req", None),
        P("req", None),
        P(),
        P(),
        P("req", None),
        P(),
        P(),
        P("req", None),
        P("tok", None),
        P(),
        P(),
        P(),
        P(None, "tok"),
        P(None, "tok"),
        P("tok", None),
    )
    out_specs = P(("req", "tok"), None)
    return jax.shard_map(local, mesh=mesh, in_specs=in_specs, out_specs=out_specs, check_vma=False)
```

profile of v0, /device:TPU:0, one launch (start us, length us, event | category | flops | bytes accessed | tf_op | source)
XLA Modules:
  0.0 253.7 jit_solution(10753798629921114018)
XLA Ops:
  6.6 0.0 copy-start.11
  6.6 0.0 all-gather.6.cloned.1.call-start
  6.6 2.0 constant_dynamic-slice_fusion.2
  8.6 0.9 pad_maximum_fusion
  9.5 0.0 all-gather.6.cloned.1.call-update
  9.5 0.0 reduce-scatter.3.cloned.1.call-start
  9.6 0.6 dynamic_slice.22
  10.8 0.0 copy-done.15
  10.9 0.2 reduce-window.8
  11.0 0.1 compare_and_fusion
  11.1 0.1 broadcast_bitcast_fusion
  11.2 1.1 fusion.39
  12.3 0.1 convert_reduce_fusion
  12.4 0.1 fusion.36
  12.6 1.8 fusion.41
  14.4 0.9 fusion.19
  15.3 67.7 %all-gather.6.cloned.1.call-done = bf16[8192,512]{1,0:T(8,128)(2,1)} async-done(((bf16[512,512]{1,0:T(8,128)(2,1)}), bf16[8192,512]{1,0:T(8,128)(2,1)}) %all-gather.6.cloned.1.call-update) | async-done | bytes 8388624 | tf_op jit(solution)/shard_map/prefix_gather/all_gather | solution.py:60
  83.0 6.2 %gather_fusion = bf16[8,512,512]{2,1,0:T(8,128)(2,1)} fusion(bf16[16,512,512]{2,1,0:T(8,128)(2,1)} %bitcast.15, s32[1024]{0:T(1024)S(1)} %pad_clamp_fusion), kind=kCustom, calls=%fused_computation | custom fusion | bytes 8388640 | tf_op jit(solution)/shard_map/prefix_gather/jit(_take)/gather | solution.py:63
  89.2 2.6 %bitcast_select_fusion = bf16[4096,512]{1,0:T(8,128)(2,1)S(1)} fusion(bf16[8,512,512]{2,1,0:T(8,128)(2,1)} %gather_fusion, pred[4096]{0:T(1024)(128)(4,1)S(1)} %bitcast.16), kind=kLoop, calls=%fused_computation.7 | loop fusion | flops 2097152 | bytes 8392704 | tf_op jit(solution)/shard_map/prefix_gather/jit(_take)/select_n | solution.py:63
  91.8 0.0 copy-start.6
  91.8 0.0 copy-start.13
  91.8 0.3 fusion.53
  92.1 0.6 copy-done.4
  92.7 0.1 copy-done.6
  92.8 0.1 copy-done.7
  92.9 1.6 fusion.54
  94.5 1.4 fusion
  95.9 2.2 copy-done.2
  98.1 9.5 %fusion.32 = f32[512,2560]{1,0:T(8,128)} fusion(bf16[256,2560]{1,0:T(8,128)(2,1)S(1)} %copy-done, bf16[512,256]{1,0:T(8,128)(2,1)} %get-tuple-element.13, bf16[4096,256]{1,0:T(8,128)(2,1)S(1)} %get-tuple-element.8, f32[512,4608]{1,0:T(8,128)} %copy-done.2, f32[512]{0:T(512)S(1)} %get-tuple-element.11, f32[512]{0:T(512)S(1)} %fusion), kind=kOutput, calls=%fused_computation.28 | convolution fusion | flops 1888747520 | bytes 18354176 | tf_op jit(solution)/shard_map/out_projection/dot_general | solution.py:95
  107.6 0.0 reduce-scatter.3.cloned.1.call-update
  107.7 0.0 all-gather.4.cloned.1.call-start
  107.7 39.6 %reduce-scatter.3.cloned.1.call-done = f32[64,2560]{1,0:T(8,128)} async-done(((f32[512,2560]{1,0:T(8,128)}), f32[64,2560]{1,0:T(8,128)}) %reduce-scatter.3.cloned.1.call-update) | async-done | bytes 655376 | tf_op jit(solution)/shard_map/out_projection/reduce_scatter | solution.py:94
  147.3 1.2 multiply_reduce_fusion.2
  148.5 1.5 multiply_reduce_fusion.1
  150.0 0.0 copy-done.9
  150.0 2.1 multiply_convert_fusion
  152.2 0.0 all-gather.4.cloned.1.call-update
  152.2 0.2 reduce-scatter.5.cloned.1.call-start
  152.4 25.6 %all-gather.4.cloned.1.call-done = bf16[512,2560]{1,0:T(8,128)(2,1)} async-done(((bf16[64,2560]{1,0:T(8,128)(2,1)}), bf16[512,2560]{1,0:T(8,128)(2,1)}) %all-gather.4.cloned.1.call-update) | async-done | bytes 2621456 | tf_op jit(solution)/shard_map/out_projection/all_gather | solution.py:103
  178.0 8.8 %fusion.55 = f32[512,1280]{1,0:T(8,128)} fusion(bf16[512,2560]{1,0:T(8,128)(2,1)} %all-gather.4.cloned.1.call-done, bf16[2560,1280]{1,0:T(8,128)(2,1)} %param.29), kind=kOutput, calls=%fused_computation.72 | convolution fusion | flops 3355443200 | bytes 11796480 | tf_op jit(solution)/shard_map/feed_forward/dot_general | solution.py:105
  186.7 16.5 %fusion.35 = f32[512,2560]{1,0:T(8,128)} fusion(bf16[1280,2560]{1,0:T(8,128)(2,1)} %param.31, bf16[512,2560]{1,0:T(8,128)(2,1)} %all-gather.4.cloned.1.call-done, bf16[2560,1280]{1,0:T(8,128)(2,1)} %param.30, f32[512,1280]{1,0:T(8,128)} %fusion.55), kind=kOutput, calls=%fused_computation.29 | convolution fusion | flops 6717440000 | bytes 23592960 | tf_op jit(solution)/shard_map/feed_forward/dot_general | solution.py:109
  203.2 0.0 reduce-scatter.5.cloned.1.call-update
  203.2 0.0 copy-start.1
  203.2 40.6 %reduce-scatter.5.cloned.1.call-done = f32[64,2560]{1,0:T(8,128)} async-done(((f32[512,2560]{1,0:T(8,128)}), f32[64,2560]{1,0:T(8,128)}) %reduce-scatter.5.cloned.1.call-update) | async-done | bytes 655376 | tf_op jit(solution)/shard_map/feed_forward/reduce_scatter | solution.py:108
  243.8 1.2 multiply_reduce_fusion
  245.0 0.0 copy-done.3
  245.0 0.0 copy-done.10
  245.0 2.2 add_convert_fusion
  (27 shorter events, 0.1 us)
Async XLA Ops:
  6.5 91.5 %copy-start = (bf16[256,2560]{1,0:T(8,128)(2,1)S(1)}, bf16[256,2560]{1,0:T(8,128)(2,1)}, u32[]{:S(2)}) copy-start(bf16[256,2560]{1,0:T(8,128)(2,1)} %param.25) | copy-start | bytes 3932164
  6.5 3.0 %copy-start.14 = (s32[16]{0:T(128)S(1)}, s32[16]{0:T(128)}, u32[]{:S(2)}) copy-start(s32[16]{0:T(128)} %param.22) | copy-start | bytes 196
  6.5 4.3 %copy-start.15 = (s32[1,3]{1,0:T(1,128)S(1)}, s32[1,3]{1,0:T(1,128)}, u32[]{:S(2)}) copy-start(s32[1,3]{1,0:T(1,128)} %param.21) | copy-start | bytes 40
  6.5 4.5 %copy-start.12 = (s32[16]{0:T(128)S(1)}, s32[16]{0:T(128)}, u32[]{:S(2)}) copy-start(s32[16]{0:T(128)} %param.23) | copy-start | bytes 196
  6.5 5.9 %copy-start.5 = (bf16[512,256]{1,0:T(8,128)(2,1)S(1)}, bf16[512,256]{1,0:T(8,128)(2,1)}, u32[]{:S(2)}) copy-start(bf16[512,256]{1,0:T(8,128)(2,1)} %param.16) | copy-start | bytes 786436
  6.6 6.0 %copy-start.11 = (f32[256]{0:T(256)S(1)}, f32[256]{0:T(256)}, u32[]{:S(2)}) copy-start(f32[256]{0:T(256)} %param.20) | copy-start | bytes 3076
  6.6 76.4 %all-gather.6.cloned.1.call-start = ((), (), s32[]{:S(2)}) async-start(), calls=%async_computation.5 | async-start | bytes 8912896 | tf_op jit(solution)/shard_map/prefix_gather/all_gather | solution.py:60
  9.5 137.8 %reduce-scatter.3.cloned.1.call-start = ((), (), s32[]{:S(2)}) async-start(), calls=%async_computation.2 | async-start | bytes 5898240 | tf_op jit(solution)/shard_map/out_projection/reduce_scatter | solution.py:94
  91.8 1.0 copy-start.4
  91.8 1.0 copy-start.6
  91.8 1.1 copy-start.7
  91.8 1.1 copy-start.13
  94.4 3.6 %copy-start.2 = (f32[512,4608]{1,0:T(8,128)}, f32[512,4608]{1,0:T(8,128)S(1)}, u32[]{:S(2)}) copy-start(f32[512,4608]{1,0:T(8,128)S(1)} %get-tuple-element.12) | copy-start | bytes 28311556
  107.6 40.9 %copy-start.8 = (f32[2560]{0:T(1024)S(1)}, f32[2560]{0:T(1024)}, u32[]{:S(2)}) copy-start(f32[2560]{0:T(1024)} %param.26) | copy-start | bytes 30724
  107.6 42.4 %copy-start.9 = (f32[2560]{0:T(1024)S(1)}, f32[2560]{0:T(1024)}, u32[]{:S(2)}) copy-start(f32[2560]{0:T(1024)} %param.27) | copy-start | bytes 30724
  107.7 70.3 %all-gather.4.cloned.1.call-start = ((), (), s32[]{:S(2)}) async-start(), calls=%async_computation.3 | async-start | bytes 2949120 | tf_op jit(solution)/shard_map/out_projection/all_gather | solution.py:103
  152.2 91.6 %reduce-scatter.5.cloned.1.call-start = ((), (), s32[]{:S(2)}) async-start(), calls=%async_computation.4 | async-start | bytes 5898240 | tf_op jit(solution)/shard_map/feed_forward/reduce_scatter | solution.py:108
  203.2 41.8 %copy-start.3 = (f32[64,2560]{1,0:T(8,128)S(1)}, f32[64,2560]{1,0:T(8,128)}, u32[]{:S(2)}) copy-start(f32[64,2560]{1,0:T(8,128)} %reduce-scatter.3.cloned.1.call-done) | copy-start | bytes 1966084
  203.2 41.8 %copy-start.10 = (f32[2560]{0:T(1024)S(1)}, f32[2560]{0:T(1024)}, u32[]{:S(2)}) copy-start(f32[2560]{0:T(1024)} %param.28) | copy-start | bytes 30724
  203.2 44.0 %copy-start.1 = (bf16[256,2560]{1,0:T(8,128)(2,1)S(1)}, bf16[256,2560]{1,0:T(8,128)(2,1)}, u32[]{:S(2)}) copy-start(bf16[256,2560]{1,0:T(8,128)(2,1)} %param.25) | copy-start | bytes 3932164
Sparse Core Ops, SparseCore 0:
  9.6 73.3 all-gather.5
  107.8 39.4 reduce-scatter.2
  152.3 25.6 all-gather.3
  203.3 40.3 reduce-scatter.4
where the time goes:
time: 254 us
  waiting for transfers between devices  173 us (68%)
  matrix products  36.3 us (14%)
  other arithmetic  17.4 us (7%)
  between operations  14 us (6%)
  local copies, waits for them, and re-layouts  12.2 us (5%)
    all_gather x1, waiting for transfers between devices, local(): gathered = lax.all_gather(pref_kv, 'req', axis=0, tiled=False)  67.7 us
    reduce_scatter x1, waiting for transfers between devices, local(): lax.psum_scatter(jnp.dot(hidden, w_down, preferred_element_type=jnp.float...  40.6 us
    reduce_scatter x1, waiting for transfers between devices, local(): lax.psum_scatter(jnp.dot(attention, w_out, preferred_element_type=jnp.flo...  39.6 us
    all_gather x1, waiting for transfers between devices, local(): normed = lax.all_gather(normed_share, 'tok', axis=0, tiled=True)  25.6 us
    dot_general x1, matrix products, local(): jnp.dot(hidden, w_down, preferred_element_type=jnp.float32)  16.5 us
    dot_general x1, matrix products, local(): jnp.dot(attention, w_out, preferred_element_type=jnp.float32)  9.55 us
    dot_general x1, matrix products, local(): gate = jnp.dot(normed, w_gate, preferred_element_type=jnp.float32)  8.76 us
    gather x1, local copies, waits for them, and re-layouts, local(): shared = jnp.take(gathered, owner_ids, axis=0).reshape(-1, 2 * HD)  6.17 us
  transfers between devices with their start and end apart: 4, of which 4 were waited for; matrix products, arithmetic and copies ran while one was open for 2% of the time, Pallas kernels for 0%

commit v1 on v0

--- a/solution.py
+++ b/solution.py
@@ -100,7 +100,9 @@
         residual_share = lax.dynamic_slice_in_dim(residual, first_row, share, 0)
         mixed_share = residual_share.astype(jnp.float32) + rms_scale(projected, attn_gain)
         normed_share = rms_scale(mixed_share, ffn_in_gain).astype(jnp.bfloat16)
-        normed = lax.all_gather(normed_share, "tok", axis=0, tiled=True)
+        normed = jnp.concatenate(
+            lax.all_to_all(jnp.stack([normed_share] * lax.axis_size("tok")), "tok", 0, 0), axis=0
+        )
     with jax.named_scope("feed_forward"):
         gate = jnp.dot(normed, w_gate, preferred_element_type=jnp.float32)
         upward = jnp.dot(normed, w_up, preferred_element_type=jnp.float32)

time: 254 us -> 263 us (1.035)
  blocking collectives: 0 us -> 35.7 us
  waiting for transfers between devices: 173 us -> 147 us
    all_to_all x0 -> x1, blocking collectives: none -> 35.7 us  [local(): lax.all_to_all(jnp.stack([normed_share] * lax.axis_size('tok')), 'tok', 0...]
    all_gather x1 -> x0, waiting for transfers between devices: 25.6 us -> none  [local(): normed = lax.all_gather(normed_share, 'tok', axis=0, tiled=True)]
  transfers between devices with their start and end apart: 4 -> 3, of which waited for: 4 -> 3; matrix products, arithmetic and copies ran while one was open for 2% -> 2% of each run, Pallas kernels for 0% -> 0%
where the time goes in v1:
time: 263 us
  waiting for transfers between devices  147 us (56%)
  blocking collectives  35.7 us (14%)
  matrix products  35.5 us (13%)
  other arithmetic  16.7 us (6%)
  between operations  14 us (5%)
  local copies, waits for them, and re-layouts  13.9 us (5%)
    all_gather x1, waiting for transfers between devices, local(): gathered = lax.all_gather(pref_kv, 'req', axis=0, tiled=False)  67.7 us
    reduce_scatter x1, waiting for transfers between devices, local(): lax.psum_scatter(jnp.dot(attention, w_out, preferred_element_type=jnp.flo...  39.6 us
    reduce_scatter x1, waiting for transfers between devices, local(): lax.psum_scatter(jnp.dot(hidden, w_down, preferred_element_type=jnp.float...  39.4 us
    all_to_all x1, blocking collectives, local(): lax.all_to_all(jnp.stack([normed_share] * lax.axis_size('tok')), 'tok', 0...  35.7 us
    dot_general x1, matrix products, local(): jnp.dot(hidden, w_down, preferred_element_type=jnp.float32)  16.5 us
    dot_general x1, matrix products, local(): jnp.dot(attention, w_out, preferred_element_type=jnp.float32)  9.55 us
    dot_general x1, matrix products, local(): gate = jnp.dot(normed, w_gate, preferred_element_type=jnp.float32)  7.96 us
    gather x1, local copies, waits for them, and re-layouts, local(): shared = jnp.take(gathered, owner_ids, axis=0).reshape(-1, 2 * HD)  6.17 us
  transfers between devices with their start and end apart: 3, of which 3 were waited for; matrix products, arithmetic and copies ran while one was open for 2% of the time, Pallas kernels for 0%

profile of v1, /device:TPU:0, one launch (start us, length us, event | category | flops | bytes accessed | tf_op | source)
XLA Modules:
  0.0 262.7 jit_solution(6977417055777922550)
XLA Ops:
  6.5 0.0 copy-start
  6.6 0.0 copy-start.12
  6.6 0.0 all-gather.3.cloned.1.call-start
  6.6 2.0 constant_dynamic-slice_fusion.2
  8.6 0.9 pad_maximum_fusion
  9.5 0.0 all-gather.3.cloned.1.call-update
  9.5 0.0 reduce-scatter.3.cloned.1.call-start
  9.6 0.0 copy-done.15
  9.6 0.6 dynamic_slice.22
  10.8 0.0 copy-done.16
  10.9 0.2 reduce-window.8
  11.0 0.1 compare_and_fusion
  11.1 0.1 broadcast_bitcast_fusion
  11.2 1.1 fusion.39
  12.3 0.1 convert_reduce_fusion
  12.4 0.1 fusion.36
  12.6 1.8 fusion.41
  14.4 0.9 fusion.19
  15.3 67.7 %all-gather.3.cloned.1.call-done = bf16[8192,512]{1,0:T(8,128)(2,1)} async-done(((bf16[512,512]{1,0:T(8,128)(2,1)}), bf16[8192,512]{1,0:T(8,128)(2,1)}) %all-gather.3.cloned.1.call-update) | async-done | bytes 8388624 | tf_op jit(solution)/shard_map/prefix_gather/all_gather | solution.py:60
  83.0 6.2 %gather_fusion = bf16[8,512,512]{2,1,0:T(8,128)(2,1)} fusion(bf16[16,512,512]{2,1,0:T(8,128)(2,1)} %bitcast.18, s32[1024]{0:T(1024)S(1)} %pad_clamp_fusion), kind=kCustom, calls=%fused_computation | custom fusion | bytes 8388640 | tf_op jit(solution)/shard_map/prefix_gather/jit(_take)/gather | solution.py:63
  89.2 2.6 bitcast_select_fusion
  91.8 0.0 copy-start.7
  91.8 0.0 copy-start.14
  91.8 0.3 fusion.53
  92.1 0.6 copy-done.5
  92.7 0.1 copy-done.7
  92.8 0.1 copy-done.8
  92.9 1.6 fusion.54
  94.5 1.4 fusion
  95.9 2.2 copy-done.2
  98.1 9.5 %fusion.32 = f32[512,2560]{1,0:T(8,128)} fusion(bf16[256,2560]{1,0:T(8,128)(2,1)S(1)} %copy-done, bf16[512,256]{1,0:T(8,128)(2,1)} %get-tuple-element.13, bf16[4096,256]{1,0:T(8,128)(2,1)S(1)} %get-tuple-element.8, f32[512,4608]{1,0:T(8,128)} %copy-done.2, f32[512]{0:T(512)S(1)} %get-tuple-element.11, f32[512]{0:T(512)S(1)} %fusion), kind=kOutput, calls=%fused_computation.28 | convolution fusion | flops 1888747520 | bytes 18354176 | tf_op jit(solution)/shard_map/out_projection/dot_general | solution.py:95
  107.6 0.0 reduce-scatter.3.cloned.1.call-update
  107.7 0.0 reduce-scatter.5.cloned.1.call-start
  107.7 39.6 %reduce-scatter.3.cloned.1.call-done = f32[64,2560]{1,0:T(8,128)} async-done(((f32[512,2560]{1,0:T(8,128)}), f32[64,2560]{1,0:T(8,128)}) %reduce-scatter.3.cloned.1.call-update) | async-done | bytes 655376 | tf_op jit(solution)/shard_map/out_projection/reduce_scatter | solution.py:94
  147.3 1.2 multiply_reduce_fusion.2
  148.5 1.5 multiply_reduce_fusion.1
  150.0 0.0 copy-done.10
  150.0 1.4 multiply_convert_fusion
  151.4 0.2 stack.2
  151.7 35.7 %all_to_all.5 = bf16[8,64,2560]{2,1,0:T(8,128)(2,1)S(1)} all-to-all(bf16[8,64,2560]{2,1,0:T(8,128)(2,1)S(1)} %stack.2), channel_id=1, replica_groups=mesh['req'=16,'tok'=8] {'tok'}, dimensions={0} | all-to-all | bytes 5242880 | tf_op jit(solution)/shard_map/out_projection/all_to_all | solution.py:104
  187.3 1.5 copy-done.4
  188.8 8.0 %fusion.55 = f32[512,1280]{1,0:T(8,128)} fusion(bf16[512,2560]{1,0:T(8,128)(2,1)S(1)} %bitcast.16, bf16[2560,1280]{1,0:T(8,128)(2,1)} %param.29), kind=kOutput, calls=%fused_computation.72 | convolution fusion | flops 3355443200 | bytes 11796480 | tf_op jit(solution)/shard_map/feed_forward/dot_general | solution.py:107
  196.8 16.5 %fusion.35 = f32[512,2560]{1,0:T(8,128)} fusion(bf16[1280,2560]{1,0:T(8,128)(2,1)} %param.31, bf16[512,2560]{1,0:T(8,128)(2,1)} %bitcast.17, bf16[2560,1280]{1,0:T(8,128)(2,1)} %param.30, f32[512,1280]{1,0:T(8,128)} %fusion.55), kind=kOutput, calls=%fused_computation.29 | convolution fusion | flops 6717440000 | bytes 23592960 | tf_op jit(solution)/shard_map/feed_forward/dot_general | solution.py:111
  213.3 0.0 reduce-scatter.5.cloned.1.call-update
  213.3 0.0 copy-start.1
  213.3 39.4 %reduce-scatter.5.cloned.1.call-done = f32[64,2560]{1,0:T(8,128)} async-done(((f32[512,2560]{1,0:T(8,128)}), f32[64,2560]{1,0:T(8,128)}) %reduce-scatter.5.cloned.1.call-update) | async-done | bytes 655376 | tf_op jit(solution)/shard_map/feed_forward/reduce_scatter | solution.py:110
  252.7 1.2 multiply_reduce_fusion
  254.0 2.2 add_convert_fusion
  (28 shorter events, 0.1 us)
Async XLA Ops:
  6.5 91.5 %copy-start = (bf16[256,2560]{1,0:T(8,128)(2,1)S(1)}, bf16[256,2560]{1,0:T(8,128)(2,1)}, u32[]{:S(2)}) copy-start(bf16[256,2560]{1,0:T(8,128)(2,1)} %param.25) | copy-start | bytes 3932164
  6.5 3.0 %copy-start.15 = (s32[16]{0:T(128)S(1)}, s32[16]{0:T(128)}, u32[]{:S(2)}) copy-start(s32[16]{0:T(128)} %param.22) | copy-start | bytes 196
  6.5 4.3 %copy-start.16 = (s32[1,3]{1,0:T(1,128)S(1)}, s32[1,3]{1,0:T(1,128)}, u32[]{:S(2)}) copy-start(s32[1,3]{1,0:T(1,128)} %param.21) | copy-start | bytes 40
  6.5 4.5 %copy-start.13 = (s32[16]{0:T(128)S(1)}, s32[16]{0:T(128)}, u32[]{:S(2)}) copy-start(s32[16]{0:T(128)} %param.23) | copy-start | bytes 196
  6.5 5.9 %copy-start.6 = (bf16[512,256]{1,0:T(8,128)(2,1)S(1)}, bf16[512,256]{1,0:T(8,128)(2,1)}, u32[]{:S(2)}) copy-start(bf16[512,256]{1,0:T(8,128)(2,1)} %param.16) | copy-start | bytes 786436
  6.6 6.0 %copy-start.12 = (f32[256]{0:T(256)S(1)}, f32[256]{0:T(256)}, u32[]{:S(2)}) copy-start(f32[256]{0:T(256)} %param.20) | copy-start | bytes 3076
  6.6 76.4 %all-gather.3.cloned.1.call-start = ((), (), s32[]{:S(2)}) async-start(), calls=%async_computation.5 | async-start | bytes 8912896 | tf_op jit(solution)/shard_map/prefix_gather/all_gather | solution.py:60
  9.5 137.8 %reduce-scatter.3.cloned.1.call-start = ((), (), s32[]{:S(2)}) async-start(), calls=%async_computation.3 | async-start | bytes 5898240 | tf_op jit(solution)/shard_map/out_projection/reduce_scatter | solution.py:94
  91.8 1.0 copy-start.5
  91.8 1.0 copy-start.7
  91.8 1.1 copy-start.8
  91.8 1.1 copy-start.14
  94.4 3.6 %copy-start.2 = (f32[512,4608]{1,0:T(8,128)}, f32[512,4608]{1,0:T(8,128)S(1)}, u32[]{:S(2)}) copy-start(f32[512,4608]{1,0:T(8,128)S(1)} %get-tuple-element.12) | copy-start | bytes 28311556
  107.6 40.9 %copy-start.9 = (f32[2560]{0:T(1024)S(1)}, f32[2560]{0:T(1024)}, u32[]{:S(2)}) copy-start(f32[2560]{0:T(1024)} %param.26) | copy-start | bytes 30724
  107.6 42.4 %copy-start.10 = (f32[2560]{0:T(1024)S(1)}, f32[2560]{0:T(1024)}, u32[]{:S(2)}) copy-start(f32[2560]{0:T(1024)} %param.27) | copy-start | bytes 30724
  107.7 145.1 %reduce-scatter.5.cloned.1.call-start = ((), (), s32[]{:S(2)}) async-start(), calls=%async_computation.4 | async-start | bytes 5898240 | tf_op jit(solution)/shard_map/feed_forward/reduce_scatter | solution.py:110
  187.3 1.5 copy-start.4
  213.2 40.7 %copy-start.3 = (f32[64,2560]{1,0:T(8,128)S(1)}, f32[64,2560]{1,0:T(8,128)}, u32[]{:S(2)}) copy-start(f32[64,2560]{1,0:T(8,128)} %reduce-scatter.3.cloned.1.call-done) | copy-start | bytes 1966084
  213.2 40.7 %copy-start.11 = (f32[2560]{0:T(1024)S(1)}, f32[2560]{0:T(1024)}, u32[]{:S(2)}) copy-start(f32[2560]{0:T(1024)} %param.28) | copy-start | bytes 30724
  213.3 42.9 %copy-start.1 = (bf16[256,2560]{1,0:T(8,128)(2,1)S(1)}, bf16[256,2560]{1,0:T(8,128)(2,1)}, u32[]{:S(2)}) copy-start(bf16[256,2560]{1,0:T(8,128)(2,1)} %param.25) | copy-start | bytes 3932164
Sparse Core Ops, SparseCore 0:
  9.6 73.3 all-gather.2
  107.8 39.4 reduce-scatter.2
  213.4 39.2 reduce-scatter.4
